TPU v7x, 128 devices: a whole 4x4x4 slice. The times are simulated.
128 devices in a mesh: dev: 128 (over x, y, z, core).
Axes of the slice: x: 4, y: 4, z: 4, core: 2. Of those that a mesh axis runs over, the one named last changes fastest.
Arguments:
- features: bfloat16 [65536, 1024], P('dev'), may hold values from -6 to 6
- w_hidden: bfloat16 [1024, 512], replicated, may hold values from -0.1875 to 0.1875
- w_out: bfloat16 [512, 128], replicated, may hold values from -0.25 to 0.25
- items: bfloat16 [262144, 128], P('dev'), may hold values from -200 to 200
- routes: int32 [65536, 4], P('dev'), may hold values from 0 to 2047, all different within a row; in each aligned block of 512 rows (0 to 511, 512 to 1023, ...) at most 2 rows name the same one
- cluster_slot: int32 [2048], replicated, may hold values from 0 to 2047, each once
- sample_ids: int32 [2048, 4096], P('dev'), may hold values from 0 to 127
- sample_counts: int32 [2048, 4096], P('dev'), may hold values from 1 to 4095
- positives: int32 [65536, 4], P('dev'), may hold values from 0 to 4095
Outputs:
- slot_loss: float32 [2048], P('dev')
- grad_hidden: float32 [1024, 512], replicated
- grad_out: float32 [512, 128], replicated
- item_grad: float32 [262144, 128], P('dev')
Inputs may be any that keep to these rules, and one draw needn't show every extreme that they name: `routes`: each row names 4 different clusters; within the rows of one device no cluster is named more than 2 times; every cluster is named by some row. `cluster_slot`: each cluster has one slot.
All inputs are finite; a program needn't handle non-finite values.
Results may differ from a plain program's by a relative error of at most 0.012.
The roundings to bfloat16 on the way count: a program that leaves them out, or rounds other values in their place, can miss the bound.
Values may be sent and summed in bfloat16 or wider, within the bound.
No kernel may reach another device: no remote copies, remote signals or barrier semaphores. Data moves between devices by JAX's collectives and lax.ppermute only.
A program may use at most 128 MiB of HBM per device.

v0:
```python
import math
import jax
import jax.numpy as jnp
from jax import lax
from jax.sharding import PartitionSpec as P


def silu_grad(value):
    sig = jax.nn.sigmoid(value)
    return sig * (1.0 + value * (1.0 - sig))


def slot_ranks(keys):
    order = jnp.argsort(keys, stable=True)
    sorted_keys = keys[order]
    first = jnp.searchsorted(sorted_keys, sorted_keys, side="left")
    ranked = jnp.arange(keys.shape[0], dtype=jnp.int32) - first
    return jnp.zeros_like(keys).at[order].set(ranked)


def score_block(queries, targets, block_items, table_ids, counts):
    item_rows = block_items.shape[1]
    picks = (
        table_ids[:, :, None] == lax.broadcasted_iota(jnp.int32, table_ids.shape + (item_rows,), 2)
    ).astype(jnp.bfloat16)
    table = jnp.einsum(
        "csi,cie->cse", picks, block_items, preferred_element_type=jnp.float32
    ).astype(jnp.bfloat16)
    scores = jnp.einsum("cqe,cse->cqs", queries, table, preferred_element_type=jnp.float32)
    scores = scores - jnp.log(counts.astype(jnp.float32))[:, None, :]
    top = jnp.max(scores, axis=2, keepdims=True)
    expo = jnp.exp(scores - top)
    total = jnp.sum(expo, axis=2, keepdims=True)
    hit = lax.broadcasted_iota(jnp.int32, scores.shape, 2) == targets[:, :, None]
    picked = jnp.sum(jnp.where(hit, scores, 0.0), axis=2)
    losses = jnp.log(total[:, :, 0]) + top[:, :, 0] - picked
    live = targets >= 0
    cluster_loss = jnp.sum(jnp.where(live, losses, 0.0), axis=1) / jnp.sum(
        live.astype(jnp.float32), axis=1
    )
    weight = (expo / total - hit.astype(jnp.float32)).astype(jnp.bfloat16)
    wsum = jnp.einsum("cqs,csi->cqi", weight, picks, preferred_element_type=jnp.float32)
    dquery = jnp.einsum(
        "cqi,cie->cqe", wsum, block_items.astype(jnp.float32), precision=lax.Precision.HIGHEST
    ).astype(jnp.bfloat16)
    dtable = jnp.einsum(
        "cqi,cqe->cie", wsum, queries.astype(jnp.float32), precision=lax.Precision.HIGHEST
    )
    return (cluster_loss, dquery, dtable)


def owner_range(got_query, got_target, items, sample_ids, sample_counts, first, count):
    local_clusters = sample_ids.shape[0]
    width = items.shape[1]
    item_rows = items.shape[0] // local_clusters
    cluster_items = items.reshape(local_clusters, item_rows, width)
    block = math.gcd(count, 4)

    def step(carry, index):
        start = first + index * block
        queries = lax.dynamic_slice_in_dim(got_query, start, block, 0)
        targets = lax.dynamic_slice_in_dim(got_target, start, block, 0)
        table_ids = lax.dynamic_slice_in_dim(sample_ids, start, block, 0)
        counts = lax.dynamic_slice_in_dim(sample_counts, start, block, 0)
        block_items = lax.dynamic_slice_in_dim(cluster_items, start, block, 0)
        cluster_loss, dquery, dtable = score_block(queries, targets, block_items, table_ids, counts)
        return (carry, (cluster_loss, dquery, dtable))

    _, (losses, dquery, dtable) = lax.scan(
        step, jnp.zeros((), jnp.float32), jnp.arange(count // block, dtype=jnp.int32)
    )
    losses = losses.reshape((count,))
    dquery = dquery.reshape((count,) + dquery.shape[2:])
    grads = dtable.reshape((count * item_rows, width))
    return (grads, losses, dquery)


def local(
    features, w_hidden, w_out, items, routes, cluster_slot, sample_ids, sample_counts, positives
):
    devices = lax.axis_size("dev")
    users, visits = routes.shape
    clusters = cluster_slot.shape[0]
    local_clusters = sample_ids.shape[0]
    width = w_out.shape[1]
    capacity = max(2, 2 * users * visits // (local_clusters * devices))
    pre = jnp.dot(features, w_hidden, preferred_element_type=jnp.float32)
    hidden = jax.nn.silu(pre).astype(jnp.bfloat16)
    query = jnp.dot(hidden, w_out, preferred_element_type=jnp.float32).astype(jnp.bfloat16)
    flat_slots = jnp.take(cluster_slot, routes.reshape(-1), axis=0)
    ranks = slot_ranks(flat_slots)
    place = flat_slots * capacity + ranks
    send_query = (
        jnp.zeros((clusters * capacity, width), jnp.bfloat16)
        .at[place]
        .set(jnp.repeat(query, visits, axis=0))
    )
    send_target = (
        jnp.full((clusters * capacity,), -1, jnp.int32).at[place].set(positives.reshape(-1))
    )
    got_query, got_target = (
        lax.all_to_all(
            send_query.reshape(clusters, capacity, width),
            "dev",
            split_axis=0,
            concat_axis=1,
            tiled=True,
        ),
        lax.all_to_all(
            send_target.reshape(clusters, capacity), "dev", split_axis=0, concat_axis=1, tiled=True
        ),
    )
    grads, slot_loss, dq_all = owner_range(
        got_query, got_target, items, sample_ids, sample_counts, 0, local_clusters
    )
    returned = lax.all_to_all(dq_all, "dev", split_axis=1, concat_axis=0, tiled=True).reshape(
        clusters * capacity, width
    )
    dq_pairs = jnp.take(returned, place, axis=0).astype(jnp.float32).reshape(users, visits, width)
    dq_total = jnp.sum(dq_pairs, axis=1).astype(jnp.bfloat16)
    local_out = jnp.dot(hidden.T, dq_total, preferred_element_type=jnp.float32)
    dhidden = jnp.dot(dq_total, w_out.T, preferred_element_type=jnp.float32)
    dpre = (dhidden * silu_grad(pre)).astype(jnp.bfloat16)
    local_hidden = jnp.dot(features.T, dpre, preferred_element_type=jnp.float32)
    grad_hidden, grad_out = lax.psum((local_hidden, local_out), "dev")
    return (slot_loss, grad_hidden, grad_out, grads)


def solution(mesh):
    in_specs = (
        P("dev", None),
        P(),
        P(),
        P("dev", None),
        P("dev", None),
        P(),
        P("dev", None),
        P("dev", None),
        P("dev", None),
    )
    out_specs = (P("dev"), P(), P(), P("dev", None))
    return jax.shard_map(local, mesh=mesh, in_specs=in_specs, out_specs=out_specs, check_vma=False)
```

profile of v0, /device:TPU:1, one launch (start us, length us, event | category | flops | bytes accessed | tf_op | source)
XLA Modules:
  0.0 579.7 jit_solution(11802738402833302580)
XLA Ops:
  8.5 10.2 %gather_fusion.1 = s32[2048]{0:T(1024)S(1)} fusion(s32[2048]{0:T(1024)} %param.18, s32[2048]{0:T(1024)S(1)} %broadcast_clamp_fusion.3), kind=kCustom, calls=%fused_computation.1 | custom fusion | bytes 24576 | tf_op jit(solution)/shard_map/jit(_take)/gather | solution.py:90
  18.8 5.0 sort.17
  23.8 11.8 %gather_fusion.2 = s32[2048]{0:T(1024)S(1)} fusion(s32[2048]{0:T(1024)S(1)} %and_select_fusion, s32[2048]{0:T(1024)S(1)} %get-tuple-element.234), kind=kCustom, calls=%fused_computation.2 | custom fusion | bytes 24576 | tf_op jit(solution)/shard_map/gather | solution.py:15
  35.6 142.4 %while.40 = (s32[]{:T(128)}, u32[2048]{0:T(1024)S(1)}, u32[2048]{0:T(1024)S(1)}, s32[2048]{0:T(1024)S(1)}, s32[]{:T(128)}, /*index=5*/s32[]{:T(128)}, s32[]{}) while((s32[]{:T(128)}, u32[2048]{0:T(1024)S(1)}, u32[2048]{0:T(1024)S(1)}, s32[2048]{0:T(1024)S(1)}, s32[]{:T(128)}, /*index=5*/s32[]{:T(128)}, s32[]{}) %tuple.75), condition=%wide.region_2.3_spmd.clone, body=%wide.region_1.2_spmd.clone.sunk | while | flops 38916 | bytes 135277 | solution.py:16
  35.7 11.8 %gather_fusion = s32[2048]{0:T(1024)S(1)} fusion(s32[2048]{0:T(1024)S(1)} %get-tuple-element.361, u32[2048]{0:T(1024)S(1)} %broadcast_clamp_fusion.5), kind=kCustom, calls=%fused_computation.clone.clone.1 | custom fusion | bytes 24576 | tf_op jit(solution)/shard_map/jit(searchsorted)/jit(_searchsorted_scan_impl)/vmap(jit(_searchsorted_scan_impl))/while/body/eval_jaxpr/gather | solution.py:16
  47.5 11.8 %gather_fusion = s32[2048]{0:T(1024)S(1)} fusion(s32[2048]{0:T(1024)S(1)} %get-tuple-element.361, u32[2048]{0:T(1024)S(1)} %broadcast_clamp_fusion.5), kind=kCustom, calls=%fused_computation.clone.clone.1 | custom fusion | bytes 24576 | tf_op jit(solution)/shard_map/jit(searchsorted)/jit(_searchsorted_scan_impl)/vmap(jit(_searchsorted_scan_impl))/while/body/eval_jaxpr/gather | solution.py:16
  59.4 11.8 %gather_fusion = s32[2048]{0:T(1024)S(1)} fusion(s32[2048]{0:T(1024)S(1)} %get-tuple-element.361, u32[2048]{0:T(1024)S(1)} %broadcast_clamp_fusion.5), kind=kCustom, calls=%fused_computation.clone.clone.1 | custom fusion | bytes 24576 | tf_op jit(solution)/shard_map/jit(searchsorted)/jit(_searchsorted_scan_impl)/vmap(jit(_searchsorted_scan_impl))/while/body/eval_jaxpr/gather | solution.py:16
  71.3 11.8 %gather_fusion = s32[2048]{0:T(1024)S(1)} fusion(s32[2048]{0:T(1024)S(1)} %get-tuple-element.361, u32[2048]{0:T(1024)S(1)} %broadcast_clamp_fusion.5), kind=kCustom, calls=%fused_computation.clone.clone.1 | custom fusion | bytes 24576 | tf_op jit(solution)/shard_map/jit(searchsorted)/jit(_searchsorted_scan_impl)/vmap(jit(_searchsorted_scan_impl))/while/body/eval_jaxpr/gather | solution.py:16
  83.1 11.8 %gather_fusion = s32[2048]{0:T(1024)S(1)} fusion(s32[2048]{0:T(1024)S(1)} %get-tuple-element.361, u32[2048]{0:T(1024)S(1)} %broadcast_clamp_fusion.5), kind=kCustom, calls=%fused_computation.clone.clone.1 | custom fusion | bytes 24576 | tf_op jit(solution)/shard_map/jit(searchsorted)/jit(_searchsorted_scan_impl)/vmap(jit(_searchsorted_scan_impl))/while/body/eval_jaxpr/gather | solution.py:16
  95.0 11.8 %gather_fusion = s32[2048]{0:T(1024)S(1)} fusion(s32[2048]{0:T(1024)S(1)} %get-tuple-element.361, u32[2048]{0:T(1024)S(1)} %broadcast_clamp_fusion.5), kind=kCustom, calls=%fused_computation.clone.clone.1 | custom fusion | bytes 24576 | tf_op jit(solution)/shard_map/jit(searchsorted)/jit(_searchsorted_scan_impl)/vmap(jit(_searchsorted_scan_impl))/while/body/eval_jaxpr/gather | solution.py:16
  106.9 11.8 %gather_fusion = s32[2048]{0:T(1024)S(1)} fusion(s32[2048]{0:T(1024)S(1)} %get-tuple-element.361, u32[2048]{0:T(1024)S(1)} %broadcast_clamp_fusion.5), kind=kCustom, calls=%fused_computation.clone.clone.1 | custom fusion | bytes 24576 | tf_op jit(solution)/shard_map/jit(searchsorted)/jit(_searchsorted_scan_impl)/vmap(jit(_searchsorted_scan_impl))/while/body/eval_jaxpr/gather | solution.py:16
  118.7 11.8 %gather_fusion = s32[2048]{0:T(1024)S(1)} fusion(s32[2048]{0:T(1024)S(1)} %get-tuple-element.361, u32[2048]{0:T(1024)S(1)} %broadcast_clamp_fusion.5), kind=kCustom, calls=%fused_computation.clone.clone.1 | custom fusion | bytes 24576 | tf_op jit(solution)/shard_map/jit(searchsorted)/jit(_searchsorted_scan_impl)/vmap(jit(_searchsorted_scan_impl))/while/body/eval_jaxpr/gather | solution.py:16
  130.6 11.8 %gather_fusion = s32[2048]{0:T(1024)S(1)} fusion(s32[2048]{0:T(1024)S(1)} %get-tuple-element.361, u32[2048]{0:T(1024)S(1)} %broadcast_clamp_fusion.5), kind=kCustom, calls=%fused_computation.clone.clone.1 | custom fusion | bytes 24576 | tf_op jit(solution)/shard_map/jit(searchsorted)/jit(_searchsorted_scan_impl)/vmap(jit(_searchsorted_scan_impl))/while/body/eval_jaxpr/gather | solution.py:16
  142.5 11.8 %gather_fusion = s32[2048]{0:T(1024)S(1)} fusion(s32[2048]{0:T(1024)S(1)} %get-tuple-element.361, u32[2048]{0:T(1024)S(1)} %broadcast_clamp_fusion.5), kind=kCustom, calls=%fused_computation.clone.clone.1 | custom fusion | bytes 24576 | tf_op jit(solution)/shard_map/jit(searchsorted)/jit(_searchsorted_scan_impl)/vmap(jit(_searchsorted_scan_impl))/while/body/eval_jaxpr/gather | solution.py:16
  154.3 11.8 %gather_fusion = s32[2048]{0:T(1024)S(1)} fusion(s32[2048]{0:T(1024)S(1)} %get-tuple-element.361, u32[2048]{0:T(1024)S(1)} %broadcast_clamp_fusion.5), kind=kCustom, calls=%fused_computation.clone.clone.1 | custom fusion | bytes 24576 | tf_op jit(solution)/shard_map/jit(searchsorted)/jit(_searchsorted_scan_impl)/vmap(jit(_searchsorted_scan_impl))/while/body/eval_jaxpr/gather | solution.py:16
  166.2 11.8 %gather_fusion = s32[2048]{0:T(1024)S(1)} fusion(s32[2048]{0:T(1024)S(1)} %get-tuple-element.361, u32[2048]{0:T(1024)S(1)} %broadcast_clamp_fusion.5), kind=kCustom, calls=%fused_computation.clone.clone.1 | custom fusion | bytes 24576 | tf_op jit(solution)/shard_map/jit(searchsorted)/jit(_searchsorted_scan_impl)/vmap(jit(_searchsorted_scan_impl))/while/body/eval_jaxpr/gather | solution.py:16
  178.1 8.0 %scatter_custom_fusion = s32[2048]{0:T(1024)S(1)} fusion(s32[2048]{0:T(1024)S(1)} %get-tuple-element.235, s32[2048]{0:T(1024)S(1)} %convert_subtract_fusion, s32[]{:T(128)} %constant.92.clone.1), kind=kCustom, calls=%fused_computation.69 | custom fusion | bytes 8196 | tf_op jit(solution)/shard_map/scatter | solution.py:18
  187.0 8.1 %scatter_custom_fusion.1 = s32[4096]{0:T(1024)S(1)} fusion(s32[2048]{0:T(1024)S(1)} %get-tuple-element.231, s32[2048]{0:T(1024)S(1)} %reshape.162, s32[]{:T(128)} %constant.103.clone.1), kind=kCustom, calls=%fused_computation.62 | custom fusion | bytes 16388 | tf_op jit(solution)/shard_map/scatter | solution.py:99
  196.1 1.5 copy.40
  197.6 11.5 %all-to-all-start = ((s32[128,16,2]{1,2,0:T(2,128)}), s32[128,16,2]{1,2,0:T(2,128)S(1)}, u32[]{:S(2)}, u32[]{:S(2)}) async-start(s32[128,16,2]{1,2,0:T(2,128)} %copy.40), calls=%async_computation | async-start | bytes 262144 | tf_op jit(solution)/shard_map/all_to_all | solution.py:109
  209.1 3.0 multiply_convert_fusion
  213.4 6.8 %scatter_custom_fusion.2 = bf16[4096,128]{1,0:T(8,128)(2,1)} fusion(s32[2048]{0:T(1024)S(1)} %get-tuple-element.231, bf16[2048,128]{1,0:T(8,128)(2,1)S(1)} %bitcast.59, bf16[]{:T(256)} %constant.94.clone.1), kind=kCustom, calls=%fused_computation.55 | custom fusion | bytes 1048578 | tf_op jit(solution)/shard_map/scatter | solution.py:96
  220.2 9.8 %all-to-all-start.1 = ((bf16[2048,2,128]{2,1,0:T(2,128)(2,1)}), bf16[2048,2,128]{2,1,0:T(2,128)(2,1)S(1)}, u32[]{:S(2)}, u32[]{:S(2)}) async-start(bf16[2048,2,128]{2,1,0:T(2,128)(2,1)} %bitcast.8), calls=%async_computation.1 | async-start | bytes 2097152 | tf_op jit(solution)/shard_map/all_to_all | solution.py:102
  230.1 19.2 %all-to-all-done.1 = bf16[2048,2,128]{2,1,0:T(2,128)(2,1)S(1)} async-done(((bf16[2048,2,128]{2,1,0:T(2,128)(2,1)}), bf16[2048,2,128]{2,1,0:T(2,128)(2,1)S(1)}, u32[]{:S(2)}, u32[]{:S(2)}) %all-to-all-start.1) | async-done | bytes 1048608 | tf_op jit(solution)/shard_map/all_to_all | solution.py:102
  249.6 131.4 %while.39 = (s32[]{:T(128)}, f32[4,4]{1,0:T(4,128)S(1)}, bf16[4,4,256,128]{3,1,0,2:T(4,128)(2,1)}, f32[4,4,128,128]{3,2,1,0:T(8,128)}, s32[4]{0:T(128)S(1)}, /*i...) while((s32[]{:T(128)}, f32[4,4]{1,0:T(4,128)S(1)}, ...), condition=%wide.region_12.13_spmd, body=%wide.region_6.12_spmd.sunk | while | flops 3156365312 | bytes 54909272 | solution.py:69
  252.9 7.5 %subtract_reduce_fusion.2 = (f32[4,256]{1,0:T(4,128)S(1)}, f32[4,256,4096]{2,1,0:T(8,128)}) fusion(f32[4,4096]{1,0:T(4,128)S(1)} %convert_log_fusion.2, s32[4,4096]{1,0:T(4,128)S(1)} %constant_dynamic-slice_fusion.6, bf16[16,128,128]{2,1,0:T(8,128)(2,1)S(1)} %get-tuple-element.401, s32[]{:T(128)S(6)} %select_n.90, ...), kind=kOutput, calls=%fused_computation.12.clone.1 | convolution fusion | flops 1623194624 | bytes 17305604 | tf_op jit(solution)/shard_map/while/body/eval_jaxpr/cqe,cse->cqs/dot_general | solution.py:29
  260.5 8.8 %fusion.58 = (f32[4,256]{1,0:T(4,128)S(1)}, f32[4,256]{1,0:T(4,128)S(1)}) fusion(f32[4,256,4096]{2,1,0:T(8,128)} %get-tuple-element.331, f32[4,256]{1,0:T(4,128)S(1)} %get-tuple-element.332, f32[4,4096]{1,0:T(4,128)S(1)} %convert_log_fusion.2, s32[4,256]{1,0:T(4,128)S(1)} %get-tuple-element.333), kind=kLoop, calls=%fused_computation.11.clone.1 | loop fusion | flops 25163776 | bytes 16859136 | tf_op jit(solution)/shard_map/while/body/eval_jaxpr/reduce_sum | solution.py:33
  269.5 10.3 %fusion.59 = f32[4,256,128]{2,1,0:T(8,128)S(1)} fusion(f32[4,256,4096]{2,1,0:T(8,128)} %get-tuple-element.331, f32[4,256]{1,0:T(4,128)S(1)} %get-tuple-element.335, s32[4,256]{1,0:T(4,128)S(1)} %get-tuple-element.333, f32[4,256]{1,0:T(4,128)S(1)} %get-tuple-element.332, f32[4,4096]{1,0:T(4,128)S(1)} %convert_log_fusion.2, ...), kind=kOutput, calls=%fused_computation.14.clone.1 | convolution fusion | flops 1105199104 | bytes 17444864 | tf_op jit(solution)/shard_map/while/body/eval_jaxpr/cqs,csi->cqi/dot_general | solution.py:42
  281.1 1.4 fusion.61
  285.8 7.5 %subtract_reduce_fusion.2 = (f32[4,256]{1,0:T(4,128)S(1)}, f32[4,256,4096]{2,1,0:T(8,128)}) fusion(f32[4,4096]{1,0:T(4,128)S(1)} %convert_log_fusion.2, s32[4,4096]{1,0:T(4,128)S(1)} %constant_dynamic-slice_fusion.6, bf16[16,128,128]{2,1,0:T(8,128)(2,1)S(1)} %get-tuple-element.401, s32[]{:T(128)S(6)} %select_n.90, ...), kind=kOutput, calls=%fused_computation.12.clone.1 | convolution fusion | flops 1623194624 | bytes 17305604 | tf_op jit(solution)/shard_map/while/body/eval_jaxpr/cqe,cse->cqs/dot_general | solution.py:29
  293.3 8.8 %fusion.58 = (f32[4,256]{1,0:T(4,128)S(1)}, f32[4,256]{1,0:T(4,128)S(1)}) fusion(f32[4,256,4096]{2,1,0:T(8,128)} %get-tuple-element.331, f32[4,256]{1,0:T(4,128)S(1)} %get-tuple-element.332, f32[4,4096]{1,0:T(4,128)S(1)} %convert_log_fusion.2, s32[4,256]{1,0:T(4,128)S(1)} %get-tuple-element.333), kind=kLoop, calls=%fused_computation.11.clone.1 | loop fusion | flops 25163776 | bytes 16859136 | tf_op jit(solution)/shard_map/while/body/eval_jaxpr/reduce_sum | solution.py:33
  302.3 10.3 %fusion.59 = f32[4,256,128]{2,1,0:T(8,128)S(1)} fusion(f32[4,256,4096]{2,1,0:T(8,128)} %get-tuple-element.331, f32[4,256]{1,0:T(4,128)S(1)} %get-tuple-element.335, s32[4,256]{1,0:T(4,128)S(1)} %get-tuple-element.333, f32[4,256]{1,0:T(4,128)S(1)} %get-tuple-element.332, f32[4,4096]{1,0:T(4,128)S(1)} %convert_log_fusion.2, ...), kind=kOutput, calls=%fused_computation.14.clone.1 | convolution fusion | flops 1105199104 | bytes 17444864 | tf_op jit(solution)/shard_map/while/body/eval_jaxpr/cqs,csi->cqi/dot_general | solution.py:42
  318.6 7.5 %subtract_reduce_fusion.2 = (f32[4,256]{1,0:T(4,128)S(1)}, f32[4,256,4096]{2,1,0:T(8,128)}) fusion(f32[4,4096]{1,0:T(4,128)S(1)} %convert_log_fusion.2, s32[4,4096]{1,0:T(4,128)S(1)} %constant_dynamic-slice_fusion.6, bf16[16,128,128]{2,1,0:T(8,128)(2,1)S(1)} %get-tuple-element.401, s32[]{:T(128)S(6)} %select_n.90, ...), kind=kOutput, calls=%fused_computation.12.clone.1 | convolution fusion | flops 1623194624 | bytes 17305604 | tf_op jit(solution)/shard_map/while/body/eval_jaxpr/cqe,cse->cqs/dot_general | solution.py:29
  326.2 8.8 %fusion.58 = (f32[4,256]{1,0:T(4,128)S(1)}, f32[4,256]{1,0:T(4,128)S(1)}) fusion(f32[4,256,4096]{2,1,0:T(8,128)} %get-tuple-element.331, f32[4,256]{1,0:T(4,128)S(1)} %get-tuple-element.332, f32[4,4096]{1,0:T(4,128)S(1)} %convert_log_fusion.2, s32[4,256]{1,0:T(4,128)S(1)} %get-tuple-element.333), kind=kLoop, calls=%fused_computation.11.clone.1 | loop fusion | flops 25163776 | bytes 16859136 | tf_op jit(solution)/shard_map/while/body/eval_jaxpr/reduce_sum | solution.py:33
  335.2 10.3 %fusion.59 = f32[4,256,128]{2,1,0:T(8,128)S(1)} fusion(f32[4,256,4096]{2,1,0:T(8,128)} %get-tuple-element.331, f32[4,256]{1,0:T(4,128)S(1)} %get-tuple-element.335, s32[4,256]{1,0:T(4,128)S(1)} %get-tuple-element.333, f32[4,256]{1,0:T(4,128)S(1)} %get-tuple-element.332, f32[4,4096]{1,0:T(4,128)S(1)} %convert_log_fusion.2, ...), kind=kOutput, calls=%fused_computation.14.clone.1 | convolution fusion | flops 1105199104 | bytes 17444864 | tf_op jit(solution)/shard_map/while/body/eval_jaxpr/cqs,csi->cqi/dot_general | solution.py:42
  346.8 1.4 fusion.61
  351.5 7.5 %subtract_reduce_fusion.2 = (f32[4,256]{1,0:T(4,128)S(1)}, f32[4,256,4096]{2,1,0:T(8,128)}) fusion(f32[4,4096]{1,0:T(4,128)S(1)} %convert_log_fusion.2, s32[4,4096]{1,0:T(4,128)S(1)} %constant_dynamic-slice_fusion.6, bf16[16,128,128]{2,1,0:T(8,128)(2,1)S(1)} %get-tuple-element.401, s32[]{:T(128)S(6)} %select_n.90, ...), kind=kOutput, calls=%fused_computation.12.clone.1 | convolution fusion | flops 1623194624 | bytes 17305604 | tf_op jit(solution)/shard_map/while/body/eval_jaxpr/cqe,cse->cqs/dot_general | solution.py:29
  359.0 8.8 %fusion.58 = (f32[4,256]{1,0:T(4,128)S(1)}, f32[4,256]{1,0:T(4,128)S(1)}) fusion(f32[4,256,4096]{2,1,0:T(8,128)} %get-tuple-element.331, f32[4,256]{1,0:T(4,128)S(1)} %get-tuple-element.332, f32[4,4096]{1,0:T(4,128)S(1)} %convert_log_fusion.2, s32[4,256]{1,0:T(4,128)S(1)} %get-tuple-element.333), kind=kLoop, calls=%fused_computation.11.clone.1 | loop fusion | flops 25163776 | bytes 16859136 | tf_op jit(solution)/shard_map/while/body/eval_jaxpr/reduce_sum | solution.py:33
  368.0 10.3 %fusion.59 = f32[4,256,128]{2,1,0:T(8,128)S(1)} fusion(f32[4,256,4096]{2,1,0:T(8,128)} %get-tuple-element.331, f32[4,256]{1,0:T(4,128)S(1)} %get-tuple-element.335, s32[4,256]{1,0:T(4,128)S(1)} %get-tuple-element.333, f32[4,256]{1,0:T(4,128)S(1)} %get-tuple-element.332, f32[4,4096]{1,0:T(4,128)S(1)} %convert_log_fusion.2, ...), kind=kOutput, calls=%fused_computation.14.clone.1 | convolution fusion | flops 1105199104 | bytes 17444864 | tf_op jit(solution)/shard_map/while/body/eval_jaxpr/cqs,csi->cqi/dot_general | solution.py:42
  381.0 4.6 all-to-all-start.2
  386.7 18.4 %all-to-all-done.2 = bf16[16,256,128]{2,0,1:T(8,128)(2,1)S(1)} async-done(((bf16[16,256,128]{2,0,1:T(8,128)(2,1)}), bf16[16,256,128]{2,0,1:T(8,128)(2,1)S(1)}, u32[]{:S(2)}, u32[]{:S(2)}) %all-to-all-start.2) | async-done | bytes 1048608 | tf_op jit(solution)/shard_map/all_to_all | solution.py:116
  405.9 6.2 %gather_fusion.3 = bf16[2048,128]{1,0:T(8,128)(2,1)S(1)} fusion(bf16[4096,128]{1,0:T(8,128)(2,1)S(1)} %bitcast.52, s32[2048]{0:T(1024)S(1)} %broadcast_clamp_fusion.1), kind=kCustom, calls=%fused_computation.3 | custom fusion | bytes 1056768 | tf_op jit(solution)/shard_map/jit(_take)/gather | solution.py:119
  412.1 2.9 select_reduce_fusion.2
  415.0 2.1 fusion.32
  417.1 3.6 convolution_bitcast_fusion.1
  421.3 147.1 %all-reduce.3.cloned.1.call-done = (f32[1024,512]{0,1:T(8,128)}, f32[512,128]{1,0:T(8,128)}) async-done(((f32[1024,512]{0,1:T(8,128)}, f32[512,128]{1,0:T(8,128)}), (f32[1024,512]{0,1:T(8,128)}, f32[512,128]{1,0:T(8,128)})) %all-reduce.3.cloned.1.call-update) | async-done | bytes 2359312 | tf_op jit(solution)/shard_map/psum | solution.py:125
  568.3 2.9 copy.47
  571.2 1.7 copy.92
  (137 shorter events, 26.9 us)
Async XLA Ops:
  7.2 201.9 %copy-start = (bf16[512,1024]{1,0:T(8,128)(2,1)S(1)}, bf16[512,1024]{1,0:T(8,128)(2,1)}, u32[]{:S(2)}) copy-start(bf16[512,1024]{1,0:T(8,128)(2,1)} %param.13) | copy-start | bytes 3145732
  35.6 151.1 %copy-start.6 = (s32[512,4]{0,1:T(4,128)S(1)}, s32[512,4]{0,1:T(4,128)}, u32[]{:S(2)}) copy-start(s32[512,4]{0,1:T(4,128)} %param.21) | copy-start | bytes 24580
  35.6 177.3 %copy-start.3 = (bf16[512,128]{1,0:T(8,128)(2,1)S(1)}, bf16[512,128]{1,0:T(8,128)(2,1)}, u32[]{:S(2)}) copy-start(bf16[512,128]{1,0:T(8,128)(2,1)} %param.15) | copy-start | bytes 393220
  178.0 71.5 %copy-start.1 = (bf16[2048,128]{1,0:T(8,128)(2,1)S(1)}, bf16[2048,128]{1,0:T(8,128)(2,1)}, u32[]{:S(2)}) copy-start(bf16[2048,128]{1,0:T(8,128)(2,1)} %param.16) | copy-start | bytes 1572868
  186.7 62.9 %copy-start.5 = (s32[2048]{0:T(1024)}, s32[2048]{0:T(1024)S(1)}, u32[]{:S(2)}) copy-start(s32[2048]{0:T(1024)S(1)} %get-tuple-element.231) | copy-start | bytes 24580
  197.6 22.6 %all-to-all-start = ((s32[128,16,2]{1,2,0:T(2,128)}), s32[128,16,2]{1,2,0:T(2,128)S(1)}, u32[]{:S(2)}, u32[]{:S(2)}) async-start(s32[128,16,2]{1,2,0:T(2,128)} %copy.40), calls=%async_computation | async-start | bytes 262144 | tf_op jit(solution)/shard_map/all_to_all | solution.py:109
  212.1 0.8 copy-start.2
  220.2 29.0 %all-to-all-start.1 = ((bf16[2048,2,128]{2,1,0:T(2,128)(2,1)}), bf16[2048,2,128]{2,1,0:T(2,128)(2,1)S(1)}, u32[]{:S(2)}, u32[]{:S(2)}) async-start(bf16[2048,2,128]{2,1,0:T(2,128)(2,1)} %bitcast.8), calls=%async_computation.1 | async-start | bytes 2097152 | tf_op jit(solution)/shard_map/all_to_all | solution.py:102
  249.6 136.1 %copy-start.7 = (pred[2048]{0:T(1024)(128)(4,1)S(1)}, pred[2048]{0:T(1024)(128)(4,1)}, u32[]{:S(2)}) copy-start(pred[2048]{0:T(1024)(128)(4,1)} %get-tuple-element.230) | copy-start | bytes 6148
  249.6 167.5 %copy-start.4 = (bf16[512,128]{1,0:T(8,128)(2,1)S(1)}, bf16[512,128]{1,0:T(8,128)(2,1)}, u32[]{:S(2)}) copy-start(bf16[512,128]{1,0:T(8,128)(2,1)} %param.15) | copy-start | bytes 393220
  381.0 24.0 %all-to-all-start.2 = ((bf16[16,256,128]{2,0,1:T(8,128)(2,1)}), bf16[16,256,128]{2,0,1:T(8,128)(2,1)S(1)}, u32[]{:S(2)}, u32[]{:S(2)}) async-start(bf16[16,256,128]{2,0,1:T(8,128)(2,1)} %bitcast.58), calls=%async_computation.2 | async-start | bytes 2097152 | tf_op jit(solution)/shard_map/all_to_all | solution.py:116
  385.6 182.7 %all-reduce.3.cloned.1.call-start = ((), (), s32[]{:S(2)}) async-start(), calls=%async_computation.3 | async-start | bytes 4718592 | tf_op jit(solution)/shard_map/psum | solution.py:125
Sparse Core Ops, SparseCore 0:
  420.8 147.4 all-reduce.2
where the time goes:
time: 581 us; the launch traced here: 580 us
  local copies, waits for them, and re-layouts  215 us (37%)
  waiting for transfers between devices  185 us (32%)
  matrix products  87.4 us (15%)
  other arithmetic  49.4 us (9%)
  starting transfers between devices  25.9 us (4%)
  between operations  14.3 us (2%)
    psum x1, waiting for transfers between devices, local(): grad_hidden, grad_out = lax.psum((local_hidden, local_out), 'dev')  147 us
    gather x12, local copies, waits for them, and re-layouts, slot_ranks(): first = jnp.searchsorted(sorted_keys, sorted_keys, side='left')  141 us
    dot_general x4, matrix products, score_block(): jnp.einsum('cqs,csi->cqi', weight, picks, preferred_element_type=jnp.floa...  41.3 us
    reduce_sum x4, other arithmetic, score_block(): total = jnp.sum(expo, axis=2, keepdims=True)  35.3 us
    dot_general x4, matrix products, score_block(): jnp.einsum('cqe,cse->cqs', queries, table, preferred_element_type=jnp.flo...  30.2 us
    all_to_all x1, waiting for transfers between devices, local(): lax.all_to_all(send_query.reshape(clusters, capacity, width), 'dev', spli...  19.2 us
    all_to_all x1, waiting for transfers between devices, local(): lax.all_to_all(dq_all, 'dev', split_axis=1, concat_axis=0, tiled=True)  18.4 us
    gather x1, local copies, waits for them, and re-layouts, slot_ranks(): sorted_keys = keys[order]  11.8 us
  transfers between devices with their start and end apart: 4, of which 3 were waited for; matrix products, arithmetic and copies ran while one was open for 2% of the time, Pallas kernels for 0%

commit v1 on v0

--- a/solution.py
+++ b/solution.py
@@ -113,9 +113,10 @@
     grads, slot_loss, dq_all = owner_range(
         got_query, got_target, items, sample_ids, sample_counts, 0, local_clusters
     )
-    returned = lax.all_to_all(dq_all, "dev", split_axis=1, concat_axis=0, tiled=True).reshape(
-        clusters * capacity, width
-    )
+    returned = jnp.concatenate(
+        lax.all_to_all(jnp.stack(jnp.split(dq_all, lax.axis_size("dev"), axis=1)), "dev", 0, 0),
+        axis=0,
+    ).reshape(clusters * capacity, width)
     dq_pairs = jnp.take(returned, place, axis=0).astype(jnp.float32).reshape(users, visits, width)
     dq_total = jnp.sum(dq_pairs, axis=1).astype(jnp.bfloat16)
     local_out = jnp.dot(hidden.T, dq_total, preferred_element_type=jnp.float32)

time: 581 us -> 773 us (1.33); the launches traced: 580 us -> 763 us
  local copies, waits for them, and re-layouts: 215 us -> 394 us
    unnamed x20 -> x147, local copies, waits for them, and re-layouts: 6.48 us -> 179 us
where the time goes in v1:
time: 773 us; the launch traced here: 763 us
  local copies, waits for them, and re-layouts  394 us (51%)
  waiting for transfers between devices  183 us (24%)
  matrix products  89.5 us (12%)
  other arithmetic  52.4 us (7%)
  starting transfers between devices  26.1 us (3%)
  between operations  14.4 us (2%)
    unnamed x147, local copies, waits for them, and re-layouts  179 us
    psum x1, waiting for transfers between devices, local(): grad_hidden, grad_out = lax.psum((local_hidden, local_out), 'dev')  147 us
    gather x12, local copies, waits for them, and re-layouts, slot_ranks(): first = jnp.searchsorted(sorted_keys, sorted_keys, side='left')  141 us
    dot_general x4, matrix products, score_block(): jnp.einsum('cqs,csi->cqi', weight, picks, preferred_element_type=jnp.floa...  41.5 us
    reduce_sum x4, other arithmetic, score_block(): total = jnp.sum(expo, axis=2, keepdims=True)  35.5 us
    dot_general x4, matrix products, score_block(): jnp.einsum('cqe,cse->cqs', queries, table, preferred_element_type=jnp.flo...  30.2 us
    all_to_all x1, waiting for transfers between devices, local(): lax.all_to_all(send_query.reshape(clusters, capacity, width), 'dev', spli...  18.6 us
    all_to_all x1, waiting for transfers between devices, local(): lax.all_to_all(jnp.stack(jnp.split(dq_all, lax.axis_size('dev'), axis=1))...  17.5 us
  transfers between devices with their start and end apart: 4, of which 3 were waited for; matrix products, arithmetic and copies ran while one was open for 2% of the time, Pallas kernels for 0%

profile of v1, /device:TPU:1, one launch (start us, length us, event | category | flops | bytes accessed | tf_op | source)
XLA Modules:
  0.0 762.8 jit_solution(16856223331083796632)
XLA Ops:
  8.5 10.2 %gather_fusion.1 = s32[2048]{0:T(1024)S(1)} fusion(s32[2048]{0:T(1024)} %param.18, s32[2048]{0:T(1024)S(1)} %broadcast_clamp_fusion.3), kind=kCustom, calls=%fused_computation.1 | custom fusion | bytes 24576 | tf_op jit(solution)/shard_map/jit(_take)/gather | solution.py:90
  18.8 5.0 sort.17
  23.8 11.8 %gather_fusion.2 = s32[2048]{0:T(1024)S(1)} fusion(s32[2048]{0:T(1024)S(1)} %and_select_fusion, s32[2048]{0:T(1024)S(1)} %get-tuple-element.234), kind=kCustom, calls=%fused_computation.2 | custom fusion | bytes 24576 | tf_op jit(solution)/shard_map/gather | solution.py:15
  35.6 142.4 %while.40 = (s32[]{:T(128)}, u32[2048]{0:T(1024)S(1)}, u32[2048]{0:T(1024)S(1)}, s32[2048]{0:T(1024)S(1)}, s32[]{:T(128)}, /*index=5*/s32[]{:T(128)}, s32[]{}) while((s32[]{:T(128)}, u32[2048]{0:T(1024)S(1)}, u32[2048]{0:T(1024)S(1)}, s32[2048]{0:T(1024)S(1)}, s32[]{:T(128)}, /*index=5*/s32[]{:T(128)}, s32[]{}) %tuple.75), condition=%wide.region_2.3_spmd.clone, body=%wide.region_1.2_spmd.clone.sunk | while | flops 38916 | bytes 135277 | solution.py:16
  35.7 11.8 %gather_fusion = s32[2048]{0:T(1024)S(1)} fusion(s32[2048]{0:T(1024)S(1)} %get-tuple-element.361, u32[2048]{0:T(1024)S(1)} %broadcast_clamp_fusion.5), kind=kCustom, calls=%fused_computation.clone.clone.1 | custom fusion | bytes 24576 | tf_op jit(solution)/shard_map/jit(searchsorted)/jit(_searchsorted_scan_impl)/vmap(jit(_searchsorted_scan_impl))/while/body/eval_jaxpr/gather | solution.py:16
  47.5 11.8 %gather_fusion = s32[2048]{0:T(1024)S(1)} fusion(s32[2048]{0:T(1024)S(1)} %get-tuple-element.361, u32[2048]{0:T(1024)S(1)} %broadcast_clamp_fusion.5), kind=kCustom, calls=%fused_computation.clone.clone.1 | custom fusion | bytes 24576 | tf_op jit(solution)/shard_map/jit(searchsorted)/jit(_searchsorted_scan_impl)/vmap(jit(_searchsorted_scan_impl))/while/body/eval_jaxpr/gather | solution.py:16
  59.4 11.8 %gather_fusion = s32[2048]{0:T(1024)S(1)} fusion(s32[2048]{0:T(1024)S(1)} %get-tuple-element.361, u32[2048]{0:T(1024)S(1)} %broadcast_clamp_fusion.5), kind=kCustom, calls=%fused_computation.clone.clone.1 | custom fusion | bytes 24576 | tf_op jit(solution)/shard_map/jit(searchsorted)/jit(_searchsorted_scan_impl)/vmap(jit(_searchsorted_scan_impl))/while/body/eval_jaxpr/gather | solution.py:16
  71.3 11.8 %gather_fusion = s32[2048]{0:T(1024)S(1)} fusion(s32[2048]{0:T(1024)S(1)} %get-tuple-element.361, u32[2048]{0:T(1024)S(1)} %broadcast_clamp_fusion.5), kind=kCustom, calls=%fused_computation.clone.clone.1 | custom fusion | bytes 24576 | tf_op jit(solution)/shard_map/jit(searchsorted)/jit(_searchsorted_scan_impl)/vmap(jit(_searchsorted_scan_impl))/while/body/eval_jaxpr/gather | solution.py:16
  83.1 11.8 %gather_fusion = s32[2048]{0:T(1024)S(1)} fusion(s32[2048]{0:T(1024)S(1)} %get-tuple-element.361, u32[2048]{0:T(1024)S(1)} %broadcast_clamp_fusion.5), kind=kCustom, calls=%fused_computation.clone.clone.1 | custom fusion | bytes 24576 | tf_op jit(solution)/shard_map/jit(searchsorted)/jit(_searchsorted_scan_impl)/vmap(jit(_searchsorted_scan_impl))/while/body/eval_jaxpr/gather | solution.py:16
  95.0 11.8 %gather_fusion = s32[2048]{0:T(1024)S(1)} fusion(s32[2048]{0:T(1024)S(1)} %get-tuple-element.361, u32[2048]{0:T(1024)S(1)} %broadcast_clamp_fusion.5), kind=kCustom, calls=%fused_computation.clone.clone.1 | custom fusion | bytes 24576 | tf_op jit(solution)/shard_map/jit(searchsorted)/jit(_searchsorted_scan_impl)/vmap(jit(_searchsorted_scan_impl))/while/body/eval_jaxpr/gather | solution.py:16
  106.9 11.8 %gather_fusion = s32[2048]{0:T(1024)S(1)} fusion(s32[2048]{0:T(1024)S(1)} %get-tuple-element.361, u32[2048]{0:T(1024)S(1)} %broadcast_clamp_fusion.5), kind=kCustom, calls=%fused_computation.clone.clone.1 | custom fusion | bytes 24576 | tf_op jit(solution)/shard_map/jit(searchsorted)/jit(_searchsorted_scan_impl)/vmap(jit(_searchsorted_scan_impl))/while/body/eval_jaxpr/gather | solution.py:16
  118.7 11.8 %gather_fusion = s32[2048]{0:T(1024)S(1)} fusion(s32[2048]{0:T(1024)S(1)} %get-tuple-element.361, u32[2048]{0:T(1024)S(1)} %broadcast_clamp_fusion.5), kind=kCustom, calls=%fused_computation.clone.clone.1 | custom fusion | bytes 24576 | tf_op jit(solution)/shard_map/jit(searchsorted)/jit(_searchsorted_scan_impl)/vmap(jit(_searchsorted_scan_impl))/while/body/eval_jaxpr/gather | solution.py:16
  130.6 11.8 %gather_fusion = s32[2048]{0:T(1024)S(1)} fusion(s32[2048]{0:T(1024)S(1)} %get-tuple-element.361, u32[2048]{0:T(1024)S(1)} %broadcast_clamp_fusion.5), kind=kCustom, calls=%fused_computation.clone.clone.1 | custom fusion | bytes 24576 | tf_op jit(solution)/shard_map/jit(searchsorted)/jit(_searchsorted_scan_impl)/vmap(jit(_searchsorted_scan_impl))/while/body/eval_jaxpr/gather | solution.py:16
  142.5 11.8 %gather_fusion = s32[2048]{0:T(1024)S(1)} fusion(s32[2048]{0:T(1024)S(1)} %get-tuple-element.361, u32[2048]{0:T(1024)S(1)} %broadcast_clamp_fusion.5), kind=kCustom, calls=%fused_computation.clone.clone.1 | custom fusion | bytes 24576 | tf_op jit(solution)/shard_map/jit(searchsorted)/jit(_searchsorted_scan_impl)/vmap(jit(_searchsorted_scan_impl))/while/body/eval_jaxpr/gather | solution.py:16
  154.3 11.8 %gather_fusion = s32[2048]{0:T(1024)S(1)} fusion(s32[2048]{0:T(1024)S(1)} %get-tuple-element.361, u32[2048]{0:T(1024)S(1)} %broadcast_clamp_fusion.5), kind=kCustom, calls=%fused_computation.clone.clone.1 | custom fusion | bytes 24576 | tf_op jit(solution)/shard_map/jit(searchsorted)/jit(_searchsorted_scan_impl)/vmap(jit(_searchsorted_scan_impl))/while/body/eval_jaxpr/gather | solution.py:16
  166.2 11.8 %gather_fusion = s32[2048]{0:T(1024)S(1)} fusion(s32[2048]{0:T(1024)S(1)} %get-tuple-element.361, u32[2048]{0:T(1024)S(1)} %broadcast_clamp_fusion.5), kind=kCustom, calls=%fused_computation.clone.clone.1 | custom fusion | bytes 24576 | tf_op jit(solution)/shard_map/jit(searchsorted)/jit(_searchsorted_scan_impl)/vmap(jit(_searchsorted_scan_impl))/while/body/eval_jaxpr/gather | solution.py:16
  178.1 8.0 %scatter_custom_fusion = s32[2048]{0:T(1024)S(1)} fusion(s32[2048]{0:T(1024)S(1)} %get-tuple-element.235, s32[2048]{0:T(1024)S(1)} %convert_subtract_fusion, s32[]{:T(128)} %constant.92.clone.1), kind=kCustom, calls=%fused_computation.325 | custom fusion | bytes 8196 | tf_op jit(solution)/shard_map/scatter | solution.py:18
  187.0 8.1 %scatter_custom_fusion.1 = s32[4096]{0:T(1024)S(1)} fusion(s32[2048]{0:T(1024)S(1)} %get-tuple-element.231, s32[2048]{0:T(1024)S(1)} %reshape.157, s32[]{:T(128)} %constant.103.clone.1), kind=kCustom, calls=%fused_computation.318 | custom fusion | bytes 16388 | tf_op jit(solution)/shard_map/scatter | solution.py:99
  196.1 1.5 copy.36
  197.6 11.5 %all-to-all-start = ((s32[128,16,2]{1,2,0:T(2,128)}), s32[128,16,2]{1,2,0:T(2,128)S(1)}, u32[]{:S(2)}, u32[]{:S(2)}) async-start(s32[128,16,2]{1,2,0:T(2,128)} %copy.36), calls=%async_computation | async-start | bytes 262144 | tf_op jit(solution)/shard_map/all_to_all | solution.py:109
  209.1 3.0 multiply_convert_fusion
  213.4 6.8 scatter_custom_fusion.2
  220.2 9.8 %all-to-all-start.1 = ((bf16[2048,2,128]{2,1,0:T(2,128)(2,1)}), bf16[2048,2,128]{2,1,0:T(2,128)(2,1)S(1)}, u32[]{:S(2)}, u32[]{:S(2)}) async-start(bf16[2048,2,128]{2,1,0:T(2,128)(2,1)} %bitcast.8), calls=%async_computation.1 | async-start | bytes 2097152 | tf_op jit(solution)/shard_map/all_to_all | solution.py:102
  230.7 18.6 %all-to-all-done.1 = bf16[2048,2,128]{2,1,0:T(2,128)(2,1)S(1)} async-done(((bf16[2048,2,128]{2,1,0:T(2,128)(2,1)}), bf16[2048,2,128]{2,1,0:T(2,128)(2,1)S(1)}, u32[]{:S(2)}, u32[]{:S(2)}) %all-to-all-start.1) | async-done | bytes 1048608 | tf_op jit(solution)/shard_map/all_to_all | solution.py:102
  250.1 141.7 %while.39 = (s32[]{:T(128)}, f32[4,4]{1,0:T(4,128)}, bf16[4,4,256,128]{3,2,1,0:T(8,128)(2,1)}, f32[4,4,128,128]{3,2,1,0:T(8,128)}, s32[4]{0:T(128)}, /*index=5*/...) while((s32[]{:T(128)}, f32[4,4]{1,0:T(4,128)}, ...), condition=%wide.region_12.13_spmd, body=%wide.region_6.12_spmd.sunk | while | flops 3156365312 | bytes 54384984 | solution.py:69
  254.9 7.5 subtract_reduce_fusion.2
  262.4 8.9 %fusion.59 = (f32[4,256]{1,0:T(4,128)S(1)}, f32[4,256]{1,0:T(4,128)S(1)}) fusion(f32[4,256,4096]{2,1,0:T(8,128)} %get-tuple-element.331, f32[4,256]{1,0:T(4,128)S(1)} %get-tuple-element.332, f32[4,4096]{1,0:T(4,128)S(1)} %convert_log_fusion.2, s32[4,256]{1,0:T(4,128)S(1)} %get-tuple-element.333), kind=kLoop, calls=%fused_computation.11.clone.1 | loop fusion | flops 25163776 | bytes 16859136 | tf_op jit(solution)/shard_map/while/body/eval_jaxpr/reduce_sum | solution.py:33
  272.7 10.4 %fusion.60 = f32[4,256,128]{2,1,0:T(8,128)S(1)} fusion(f32[4,256,4096]{2,1,0:T(8,128)} %get-tuple-element.331, f32[4,256]{1,0:T(4,128)S(1)} %get-tuple-element.335, s32[4,256]{1,0:T(4,128)S(1)} %get-tuple-element.333, f32[4,256]{1,0:T(4,128)S(1)} %get-tuple-element.332, f32[4,4096]{1,0:T(4,128)S(1)} %convert_log_fusion.2, ...), kind=kOutput, calls=%fused_computation.14.clone.1 | convolution fusion | flops 1105199104 | bytes 17444864 | tf_op jit(solution)/shard_map/while/body/eval_jaxpr/cqs,csi->cqi/dot_general | solution.py:42
  290.3 7.5 subtract_reduce_fusion.2
  297.8 8.9 %fusion.59 = (f32[4,256]{1,0:T(4,128)S(1)}, f32[4,256]{1,0:T(4,128)S(1)}) fusion(f32[4,256,4096]{2,1,0:T(8,128)} %get-tuple-element.331, f32[4,256]{1,0:T(4,128)S(1)} %get-tuple-element.332, f32[4,4096]{1,0:T(4,128)S(1)} %convert_log_fusion.2, s32[4,256]{1,0:T(4,128)S(1)} %get-tuple-element.333), kind=kLoop, calls=%fused_computation.11.clone.1 | loop fusion | flops 25163776 | bytes 16859136 | tf_op jit(solution)/shard_map/while/body/eval_jaxpr/reduce_sum | solution.py:33
  308.1 10.4 %fusion.60 = f32[4,256,128]{2,1,0:T(8,128)S(1)} fusion(f32[4,256,4096]{2,1,0:T(8,128)} %get-tuple-element.331, f32[4,256]{1,0:T(4,128)S(1)} %get-tuple-element.335, s32[4,256]{1,0:T(4,128)S(1)} %get-tuple-element.333, f32[4,256]{1,0:T(4,128)S(1)} %get-tuple-element.332, f32[4,4096]{1,0:T(4,128)S(1)} %convert_log_fusion.2, ...), kind=kOutput, calls=%fused_computation.14.clone.1 | convolution fusion | flops 1105199104 | bytes 17444864 | tf_op jit(solution)/shard_map/while/body/eval_jaxpr/cqs,csi->cqi/dot_general | solution.py:42
  325.7 7.5 subtract_reduce_fusion.2
  333.2 8.9 %fusion.59 = (f32[4,256]{1,0:T(4,128)S(1)}, f32[4,256]{1,0:T(4,128)S(1)}) fusion(f32[4,256,4096]{2,1,0:T(8,128)} %get-tuple-element.331, f32[4,256]{1,0:T(4,128)S(1)} %get-tuple-element.332, f32[4,4096]{1,0:T(4,128)S(1)} %convert_log_fusion.2, s32[4,256]{1,0:T(4,128)S(1)} %get-tuple-element.333), kind=kLoop, calls=%fused_computation.11.clone.1 | loop fusion | flops 25163776 | bytes 16859136 | tf_op jit(solution)/shard_map/while/body/eval_jaxpr/reduce_sum | solution.py:33
  343.5 10.4 %fusion.60 = f32[4,256,128]{2,1,0:T(8,128)S(1)} fusion(f32[4,256,4096]{2,1,0:T(8,128)} %get-tuple-element.331, f32[4,256]{1,0:T(4,128)S(1)} %get-tuple-element.335, s32[4,256]{1,0:T(4,128)S(1)} %get-tuple-element.333, f32[4,256]{1,0:T(4,128)S(1)} %get-tuple-element.332, f32[4,4096]{1,0:T(4,128)S(1)} %convert_log_fusion.2, ...), kind=kOutput, calls=%fused_computation.14.clone.1 | convolution fusion | flops 1105199104 | bytes 17444864 | tf_op jit(solution)/shard_map/while/body/eval_jaxpr/cqs,csi->cqi/dot_general | solution.py:42
  361.1 7.5 subtract_reduce_fusion.2
  368.6 8.9 %fusion.59 = (f32[4,256]{1,0:T(4,128)S(1)}, f32[4,256]{1,0:T(4,128)S(1)}) fusion(f32[4,256,4096]{2,1,0:T(8,128)} %get-tuple-element.331, f32[4,256]{1,0:T(4,128)S(1)} %get-tuple-element.332, f32[4,4096]{1,0:T(4,128)S(1)} %convert_log_fusion.2, s32[4,256]{1,0:T(4,128)S(1)} %get-tuple-element.333), kind=kLoop, calls=%fused_computation.11.clone.1 | loop fusion | flops 25163776 | bytes 16859136 | tf_op jit(solution)/shard_map/while/body/eval_jaxpr/reduce_sum | solution.py:33
  378.9 10.4 %fusion.60 = f32[4,256,128]{2,1,0:T(8,128)S(1)} fusion(f32[4,256,4096]{2,1,0:T(8,128)} %get-tuple-element.331, f32[4,256]{1,0:T(4,128)S(1)} %get-tuple-element.335, s32[4,256]{1,0:T(4,128)S(1)} %get-tuple-element.333, f32[4,256]{1,0:T(4,128)S(1)} %get-tuple-element.332, f32[4,4096]{1,0:T(4,128)S(1)} %convert_log_fusion.2, ...), kind=kOutput, calls=%fused_computation.14.clone.1 | convolution fusion | flops 1105199104 | bytes 17444864 | tf_op jit(solution)/shard_map/while/body/eval_jaxpr/cqs,csi->cqi/dot_general | solution.py:42
  423.1 1.4 constant_dynamic-update-slice_fusion.104
  508.8 1.4 constant_dynamic-update-slice_fusion.41
  559.1 1.4 constant_dynamic-update-slice_fusion.4
  566.0 4.6 all-to-all-start.2
  572.5 17.5 %all-to-all-done.2 = bf16[128,16,2,128]{3,2,1,0:T(2,128)(2,1)S(1)} async-done(((bf16[128,16,2,128]{3,2,1,0:T(2,128)(2,1)}), bf16[128,16,2,128]{3,2,1,0:T(2,128)(2,1)S(1)}, u32[]{:S(2)}, u32[]{:S(2)}) %all-to-all-start.2) | async-done | bytes 1048608 | tf_op jit(solution)/shard_map/all_to_all | solution.py:117
  590.0 6.2 gather_fusion.3
  596.2 2.9 select_reduce_fusion.2
  600.2 3.6 convolution_bitcast_fusion.1
  604.4 147.0 %all-reduce.3.cloned.1.call-done = (f32[1024,512]{0,1:T(8,128)}, f32[512,128]{1,0:T(8,128)}) async-done(((f32[1024,512]{0,1:T(8,128)}, f32[512,128]{1,0:T(8,128)}), (f32[1024,512]{0,1:T(8,128)}, f32[512,128]{1,0:T(8,128)})) %all-reduce.3.cloned.1.call-update) | async-done | bytes 2359312 | tf_op jit(solution)/shard_map/psum | solution.py:126
  751.4 2.9 copy.41
  754.3 1.7 copy.207
  (260 shorter events, 211.5 us)
Async XLA Ops:
  7.2 201.9 %copy-start = (bf16[512,1024]{1,0:T(8,128)(2,1)S(1)}, bf16[512,1024]{1,0:T(8,128)(2,1)}, u32[]{:S(2)}) copy-start(bf16[512,1024]{1,0:T(8,128)(2,1)} %param.13) | copy-start | bytes 3145732
  35.6 151.1 %copy-start.6 = (s32[512,4]{0,1:T(4,128)S(1)}, s32[512,4]{0,1:T(4,128)}, u32[]{:S(2)}) copy-start(s32[512,4]{0,1:T(4,128)} %param.21) | copy-start | bytes 24580
  35.6 177.3 %copy-start.4 = (bf16[512,128]{1,0:T(8,128)(2,1)S(1)}, bf16[512,128]{1,0:T(8,128)(2,1)}, u32[]{:S(2)}) copy-start(bf16[512,128]{1,0:T(8,128)(2,1)} %param.15) | copy-start | bytes 393220
  178.0 72.1 %copy-start.1 = (bf16[2048,128]{1,0:T(8,128)(2,1)S(1)}, bf16[2048,128]{1,0:T(8,128)(2,1)}, u32[]{:S(2)}) copy-start(bf16[2048,128]{1,0:T(8,128)(2,1)} %param.16) | copy-start | bytes 1572868
  186.7 63.4 %copy-start.5 = (s32[2048]{0:T(1024)}, s32[2048]{0:T(1024)S(1)}, u32[]{:S(2)}) copy-start(s32[2048]{0:T(1024)S(1)} %get-tuple-element.231) | copy-start | bytes 24580
  197.6 22.6 %all-to-all-start = ((s32[128,16,2]{1,2,0:T(2,128)}), s32[128,16,2]{1,2,0:T(2,128)S(1)}, u32[]{:S(2)}, u32[]{:S(2)}) async-start(s32[128,16,2]{1,2,0:T(2,128)} %copy.36), calls=%async_computation | async-start | bytes 262144 | tf_op jit(solution)/shard_map/all_to_all | solution.py:109
  212.1 0.8 copy-start.2
  220.2 29.0 %all-to-all-start.1 = ((bf16[2048,2,128]{2,1,0:T(2,128)(2,1)}), bf16[2048,2,128]{2,1,0:T(2,128)(2,1)S(1)}, u32[]{:S(2)}, u32[]{:S(2)}) async-start(bf16[2048,2,128]{2,1,0:T(2,128)(2,1)} %bitcast.8), calls=%async_computation.1 | async-start | bytes 2097152 | tf_op jit(solution)/shard_map/all_to_all | solution.py:102
  250.1 349.0 %copy-start.3 = (bf16[512,512]{1,0:T(8,128)(2,1)S(1)}, bf16[512,512]{1,0:T(8,128)(2,1)}, u32[]{:S(2)}) copy-start(bf16[512,512]{1,0:T(8,128)(2,1)} %copy-done.2) | copy-start | bytes 1572868
  391.8 212.1 %copy-start.7 = (f32[4,4]{1,0:T(4,128)S(1)}, f32[4,4]{1,0:T(4,128)}, u32[]{:S(2)}) copy-start(f32[4,4]{1,0:T(4,128)} %get-tuple-element.128) | copy-start | bytes 196
  566.0 24.0 %all-to-all-start.2 = ((bf16[128,16,2,128]{3,2,1,0:T(2,128)(2,1)}), bf16[128,16,2,128]{3,2,1,0:T(2,128)(2,1)S(1)}, u32[]{:S(2)}, u32[]{:S(2)}) async-start(bf16[128,16,2,128]{3,2,1,0:T(2,128)(2,1)} %constant_dynamic-update-slice_fusion), calls=%async_computation.2 | async-start | bytes 2097152 | tf_op jit(solution)/shard_map/all_to_all | solution.py:117
  570.6 180.9 %all-reduce.3.cloned.1.call-start = ((), (), s32[]{:S(2)}) async-start(), calls=%async_computation.3 | async-start | bytes 4718592 | tf_op jit(solution)/shard_map/psum | solution.py:126
Sparse Core Ops, SparseCore 0:
  603.9 147.4 all-reduce.2
